TPU v7x, 512 devices: a whole 4x8x8 slice. The times are simulated.
512 devices in a mesh: dp: 16 (over z, core), tp: 4 (over y_lo), cp: 8 (over y_hi, x).
Axes of the slice: x: 4, y: 8 (y_hi: 2, y_lo: 4; y = y_hi * 4 + y_lo), z: 8, core: 2. Of those that a mesh axis runs over, the one named last changes fastest.
Arguments:
- tokens: bfloat16 [65536, 1024], P(('dp', 'tp', 'cp')), may hold values from -6 to 6
- expert_ids: int32 [65536, 2], P(('dp', 'tp', 'cp')), may hold values from 0 to 31, all different within a row; in each aligned block of 128 rows (0 to 127, 128 to 255, ...) at most 12 rows name the same one
- router_weight: bfloat16 [1024, 32], replicated, may hold values from -0.1875 to 0.1875
- gate_weight: bfloat16 [32, 1024, 384], P(('tp', 'cp'), 'dp'), may hold values from -0.1875 to 0.1875
- up_weight: bfloat16 [32, 1024, 384], P(('tp', 'cp'), 'dp'), may hold values from -0.1875 to 0.1875
- down_weight: bfloat16 [32, 384, 1024], P(('tp', 'cp'), None, 'dp'), may hold values from -0.3125 to 0.3125
- grad_out: bfloat16 [65536, 1024], P(('dp', 'tp', 'cp')), may hold values from -6 to 6
Outputs:
- moe_out: bfloat16 [65536, 1024], P(('dp', 'tp', 'cp'))
- grad_tokens: bfloat16 [65536, 1024], P(('dp', 'tp', 'cp'))
- router_grad: float32 [1024, 32], replicated
Inputs may be any that keep to these rules, and one draw needn't show every extreme that they name: `expert_ids`: each row names 2 different experts. Among the 128 rows of one device no expert is named by more than 12 rows, a bound that some block reaches.
All inputs are finite; a program needn't handle non-finite values.
Results may differ from a plain program's by a relative error of at most 0.0064.
Values may be sent and summed in bfloat16 or wider, within the bound.
A program may use at most 64 MiB of HBM per device.

v0:
```python
import jax
import jax.numpy as jnp
from jax import lax
from jax.sharding import PartitionSpec as P


def route_slots(flat_ids, expert_count):
    hits = (flat_ids[:, None] == jnp.arange(expert_count, dtype=jnp.int32)[None, :]).astype(
        jnp.int32
    )
    before = jnp.cumsum(hits, axis=0) - hits
    return jnp.sum(before * hits, axis=1)


def trade(stacked, capacity):
    item_count = stacked.shape[0]
    feature_dim = stacked.shape[2]
    tp_count = lax.axis_size("tp")
    cp_count = lax.axis_size("cp")
    shaped = stacked.reshape(item_count, tp_count * cp_count, capacity, feature_dim)
    moved = lax.all_to_all(shaped, ("tp", "cp"), split_axis=1, concat_axis=1, tiled=True)
    return moved.reshape(item_count, -1, feature_dim)


def expert_forward(received, w_gate, w_up, w_down):
    gate_act = jnp.dot(received, w_gate, preferred_element_type=jnp.float32)
    up_act = jnp.dot(received, w_up, preferred_element_type=jnp.float32)
    hidden = (jax.nn.silu(gate_act) * up_act).astype(jnp.bfloat16)
    produced = jnp.dot(hidden, w_down, preferred_element_type=jnp.float32).astype(jnp.bfloat16)
    return (gate_act, up_act, produced)


def expert_backward(received_grad, gate_act, up_act, w_gate, w_up, w_down):
    contract = (((1,), (1,)), ((), ()))
    grad_hidden = lax.dot_general(
        received_grad, w_down, contract, preferred_element_type=jnp.float32
    )
    sigma = jax.nn.sigmoid(gate_act)
    grad_gate = (grad_hidden * up_act * sigma * (1.0 + gate_act * (1.0 - sigma))).astype(
        jnp.bfloat16
    )
    grad_up = (grad_hidden * gate_act * sigma).astype(jnp.bfloat16)
    returned = lax.dot_general(grad_gate, w_gate, contract, preferred_element_type=jnp.float32)
    returned = returned + lax.dot_general(
        grad_up, w_up, contract, preferred_element_type=jnp.float32
    )
    return returned.astype(jnp.bfloat16)


def on_device(tokens, expert_ids, router_weight, gate_weight, up_weight, down_weight, grad_out):
    row_count, feature_dim = tokens.shape
    topk = expert_ids.shape[1]
    groups = lax.axis_size(("tp", "cp"))
    capacity = 3 * row_count * topk // (2 * groups)
    expert_count = router_weight.shape[1]
    contract = (((1,), (1,)), ((), ()))
    w_gate, w_up, w_down = (
        lax.all_gather(gate_weight[0], "dp", axis=0, tiled=True),
        lax.all_gather(up_weight[0], "dp", axis=0, tiled=True),
        lax.all_gather(down_weight[0], "dp", axis=1, tiled=True),
    )
    logits = jnp.dot(tokens, router_weight, preferred_element_type=jnp.float32)
    chosen = jnp.take_along_axis(logits, expert_ids, axis=1)
    mixing = 1.0 / jnp.sum(jnp.exp(chosen[:, None, :] - chosen[:, :, None]), axis=2)
    flat_ids = expert_ids.reshape(-1)
    slots = route_slots(flat_ids, expert_count)
    position = flat_ids * capacity + slots
    slot_total = groups * capacity
    repeated = jnp.repeat(tokens, topk, axis=0)
    scaled_grad = (mixing[:, :, None] * grad_out.astype(jnp.float32)[:, None, :]).astype(
        jnp.bfloat16
    )
    scaled_flat = scaled_grad.reshape(-1, feature_dim)
    sent = jnp.zeros((1, slot_total, feature_dim), jnp.bfloat16).at[0, position].set(repeated)
    received = trade(sent, capacity)[0]
    gate_act, up_act, produced = expert_forward(received, w_gate, w_up, w_down)
    came_back = trade(produced[None], capacity)[0]
    sent_grad = (
        jnp.zeros((1, slot_total, feature_dim), jnp.bfloat16).at[0, position].set(scaled_flat)
    )
    received_grad = trade(sent_grad, capacity)[0]
    returned = expert_backward(received_grad, gate_act, up_act, w_gate, w_up, w_down)
    back_home = trade(returned[None], capacity)[0]
    out_rows = jnp.take(came_back, position, axis=0).reshape(row_count, topk, feature_dim)
    moe_out = jnp.sum(mixing[:, :, None] * out_rows.astype(jnp.float32), axis=1).astype(
        jnp.bfloat16
    )
    back_rows = jnp.take(back_home, position, axis=0).reshape(row_count, topk, feature_dim)
    scores = jnp.einsum("td,tkd->tk", grad_out, out_rows, preferred_element_type=jnp.float32)
    dlogit = mixing * (scores - jnp.sum(mixing * scores, axis=1, keepdims=True))
    onehot = (
        expert_ids[:, :, None] == jnp.arange(expert_count, dtype=jnp.int32)[None, None, :]
    ).astype(jnp.float32)
    dense = jnp.sum(onehot * dlogit[:, :, None], axis=1).astype(jnp.bfloat16)
    router_back = lax.dot_general(
        dense, router_weight, contract, preferred_element_type=jnp.float32
    )
    grad_tokens = (jnp.sum(back_rows.astype(jnp.float32), axis=1) + router_back).astype(
        jnp.bfloat16
    )
    router_part = lax.dot_general(
        tokens, dense, (((0,), (0,)), ((), ())), preferred_element_type=jnp.float32
    )
    router_grad = lax.psum(router_part, ("dp", "tp", "cp"))
    return (moe_out, grad_tokens, router_grad)


def solution(mesh):
    in_specs = (
        P(("dp", "tp", "cp"), None),
        P(("dp", "tp", "cp"), None),
        P(),
        P(("tp", "cp"), "dp", None),
        P(("tp", "cp"), "dp", None),
        P(("tp", "cp"), None, "dp"),
        P(("dp", "tp", "cp"), None),
    )
    out_specs = (P(("dp", "tp", "cp"), None), P(("dp", "tp", "cp"), None), P())
    return jax.shard_map(
        on_device, mesh=mesh, in_specs=in_specs, out_specs=out_specs, check_vma=False
    )
```

profile of v0, /device:TPU:1, one launch (start us, length us, event | category | flops | bytes accessed | tf_op | source)
XLA Modules:
  0.0 453.8 jit_solution(12045069232960749352)
XLA Ops:
  7.2 0.7 broadcast_multiply_fusion
  7.9 0.8 copy.57
  10.1 1.2 broadcast_in_dim.16
  11.6 1.9 scatter_custom_fusion
  13.5 1.2 reshape.105
  14.7 10.6 %all-to-all-start = ((bf16[1,32,12,1024]{3,2,0,1:T(8,128)(2,1)}), bf16[1,32,12,1024]{3,2,0,1:T(8,128)(2,1)S(1)}, u32[]{:S(2)}, u32[]{:S(2)}) async-start(bf16[1,32,12,1024]{3,2,0,1:T(8,128)(2,1)} %bitcast.4), calls=%async_computation | async-start | bytes 2097152 | tf_op jit(solution)/shard_map/all_to_all | solution.py:21
  25.3 27.5 %all-gather.2 = bf16[1,384,1024]{1,2,0:T(8,128)(2,1)} all-gather(bf16[1,384,64]{1,2,0:T(8,128)(2,1)S(1)} %copy-done.15), channel_id=4, replica_groups=mesh['dp'=16,'tp'=4,'cp'=8] {'dp'}, dimensions={2}, use_global_device_ids=true | all-gather | bytes 835584 | tf_op jit(solution)/shard_map/all_gather | solution.py:60
  52.9 16.6 %all-gather.1 = bf16[1,1024,384]{2,1,0:T(8,128)(2,1)S(1)} all-gather(bf16[1,64,384]{2,1,0:T(8,128)(2,1)S(1)} %copy-done.16), channel_id=3, replica_groups=mesh['dp'=16,'tp'=4,'cp'=8] {'dp'}, dimensions={1}, use_global_device_ids=true | all-gather | bytes 835584 | tf_op jit(solution)/shard_map/all_gather | solution.py:59
  69.5 17.9 %all-gather = bf16[1,1024,384]{2,1,0:T(8,128)(2,1)S(1)} all-gather(bf16[1,64,384]{2,1,0:T(8,128)(2,1)S(1)} %copy-done.17), channel_id=2, replica_groups=mesh['dp'=16,'tp'=4,'cp'=8] {'dp'}, dimensions={1}, use_global_device_ids=true | all-gather | bytes 835584 | tf_op jit(solution)/shard_map/all_gather | solution.py:58
  89.1 0.8 copy-done.10
  90.5 1.2 reshape_broadcast_in_dim.6
  91.8 9.6 %all-to-all-start.1 = ((bf16[1,32,12,1024]{3,2,0,1:T(8,128)(2,1)}), bf16[1,32,12,1024]{3,2,0,1:T(8,128)(2,1)S(1)}, u32[]{:S(2)}, u32[]{:S(2)}) async-start(bf16[1,32,12,1024]{3,2,0,1:T(8,128)(2,1)} %bitcast.8), calls=%async_computation.1 | async-start | bytes 2097152 | tf_op jit(solution)/shard_map/all_to_all | solution.py:21
  101.9 2.0 gather_fusion
  104.4 1.7 mul.98
  106.1 21.9 %all-to-all-done.1 = bf16[1,32,12,1024]{3,2,0,1:T(8,128)(2,1)S(1)} async-done(((bf16[1,32,12,1024]{3,2,0,1:T(8,128)(2,1)}), bf16[1,32,12,1024]{3,2,0,1:T(8,128)(2,1)S(1)}, u32[]{:S(2)}, u32[]{:S(2)}) %all-to-all-start.1) | async-done | bytes 786464 | tf_op jit(solution)/shard_map/all_to_all | solution.py:21
  128.3 1.2 gather_fusion.1
  129.8 1.1 fusion.13
  131.3 2.0 scatter_custom_fusion.1
  133.5 33.6 %all_to_all.20 = bf16[1,32,12,1024]{3,2,0,1:T(8,128)(2,1)S(1)} all-to-all(bf16[1,32,12,1024]{3,2,0,1:T(8,128)(2,1)S(1)} %bitcast.72), channel_id=1, replica_groups=mesh['dp'=16,'tp'=4,'cp'=8] {'tp','cp'}, dimensions={1} | all-to-all | bytes 1572864 | tf_op jit(solution)/shard_map/all_to_all | solution.py:21
  167.3 1.8 fusion.1
  169.1 0.7 fusion.7
  170.9 1.2 reshape_broadcast_in_dim.7
  172.1 6.0 %all-to-all-start.3 = ((bf16[1,32,12,1024]{3,2,0,1:T(8,128)(2,1)}), bf16[1,32,12,1024]{3,2,0,1:T(8,128)(2,1)S(1)}, u32[]{:S(2)}, u32[]{:S(2)}) async-start(bf16[1,32,12,1024]{3,2,0,1:T(8,128)(2,1)} %bitcast.10), calls=%async_computation.3 | async-start | bytes 2097152 | tf_op jit(solution)/shard_map/all_to_all | solution.py:21
  178.2 0.8 convolution_bitcast_fusion
  179.0 2.1 multiply_reduce_fusion
  181.2 22.9 %all-to-all-done.3 = bf16[1,32,12,1024]{3,2,0,1:T(8,128)(2,1)S(1)} async-done(((bf16[1,32,12,1024]{3,2,0,1:T(8,128)(2,1)}), bf16[1,32,12,1024]{3,2,0,1:T(8,128)(2,1)S(1)}, u32[]{:S(2)}, u32[]{:S(2)}) %all-to-all-start.3) | async-done | bytes 786464 | tf_op jit(solution)/shard_map/all_to_all | solution.py:21
  204.2 1.2 gather_fusion.2
  205.5 0.6 reshape.108
  206.1 1.2 reduce_sum.60
  207.4 1.0 fusion
  208.3 237.0 %all-reduce.3.cloned.1.call-done = f32[1024,32]{0,1:T(8,128)} async-done(((f32[1024,32]{0,1:T(8,128)}), f32[1024,32]{0,1:T(8,128)}) %all-reduce.3.cloned.1.call-update) | async-done | bytes 131088 | tf_op jit(solution)/shard_map/psum | solution.py:104
  445.3 1.6 copy.73
  (81 shorter events, 7.6 us)
Async XLA Ops:
  7.2 94.5 %copy-start = (bf16[1024,32]{0,1:T(8,128)(2,1)S(1)}, bf16[1024,32]{0,1:T(8,128)(2,1)}, u32[]{:S(2)}) copy-start(bf16[1024,32]{0,1:T(8,128)(2,1)} %param.11) | copy-start | bytes 196612
  13.5 11.8 %copy-start.15 = (bf16[1,384,64]{1,2,0:T(8,128)(2,1)S(1)}, bf16[1,384,64]{1,2,0:T(8,128)(2,1)}, u32[]{:S(2)}) copy-start(bf16[1,384,64]{1,2,0:T(8,128)(2,1)} %param.14) | copy-start | bytes 147460
  14.7 38.2 %copy-start.16 = (bf16[1,64,384]{2,1,0:T(8,128)(2,1)S(1)}, bf16[1,64,384]{2,1,0:T(8,128)(2,1)}, u32[]{:S(2)}) copy-start(bf16[1,64,384]{2,1,0:T(8,128)(2,1)} %param.13) | copy-start | bytes 147460
  14.7 54.8 %copy-start.17 = (bf16[1,64,384]{2,1,0:T(8,128)(2,1)S(1)}, bf16[1,64,384]{2,1,0:T(8,128)(2,1)}, u32[]{:S(2)}) copy-start(bf16[1,64,384]{2,1,0:T(8,128)(2,1)} %param.12) | copy-start | bytes 147460
  14.7 72.7 %all-to-all-start = ((bf16[1,32,12,1024]{3,2,0,1:T(8,128)(2,1)}), bf16[1,32,12,1024]{3,2,0,1:T(8,128)(2,1)S(1)}, u32[]{:S(2)}, u32[]{:S(2)}) async-start(bf16[1,32,12,1024]{3,2,0,1:T(8,128)(2,1)} %bitcast.4), calls=%async_computation | async-start | bytes 2097152 | tf_op jit(solution)/shard_map/all_to_all | solution.py:21
  69.5 18.7 %copy-start.2 = (bf16[1,1024,384]{2,1,0:T(8,128)(2,1)}, bf16[1,1024,384]{2,1,0:T(8,128)(2,1)S(1)}, u32[]{:S(2)}) copy-start(bf16[1,1024,384]{2,1,0:T(8,128)(2,1)S(1)} %all-gather.1) | copy-start | bytes 2359300
  87.4 0.9 copy-start.4
  88.3 0.8 copy-start.12
  88.3 1.6 copy-start.6
  89.1 0.8 copy-start.10
  90.5 10.9 %copy-start.18 = (s32[128,2]{0,1:T(2,128)S(1)}, s32[128,2]{0,1:T(2,128)}, u32[]{:S(2)}) copy-start(s32[128,2]{0,1:T(2,128)} %param.10) | copy-start | bytes 3076
  91.8 9.9 %copy-start.7 = (bf16[128,1024]{1,0:T(8,128)(2,1)S(1)}, bf16[128,1024]{1,0:T(8,128)(2,1)}, u32[]{:S(2)}) copy-start(bf16[128,1024]{1,0:T(8,128)(2,1)} %param.9) | copy-start | bytes 786436
  91.8 36.3 %all-to-all-start.1 = ((bf16[1,32,12,1024]{3,2,0,1:T(8,128)(2,1)}), bf16[1,32,12,1024]{3,2,0,1:T(8,128)(2,1)S(1)}, u32[]{:S(2)}, u32[]{:S(2)}) async-start(bf16[1,32,12,1024]{3,2,0,1:T(8,128)(2,1)} %bitcast.8), calls=%async_computation.1 | async-start | bytes 2097152 | tf_op jit(solution)/shard_map/all_to_all | solution.py:21
  101.9 2.2 copy-start.14
  129.8 1.2 copy-start.8
  129.8 1.5 copy-start.1
  167.1 2.0 copy-start.5
  167.3 1.8 copy-start.11
  167.3 1.8 copy-start.13
  169.1 1.1 copy-start.3
  172.1 6.9 %copy-start.9 = (bf16[128,2,1024]{2,1,0:T(2,128)(2,1)S(1)}, bf16[128,2,1024]{2,1,0:T(2,128)(2,1)}, u32[]{:S(2)}) copy-start(bf16[128,2,1024]{2,1,0:T(2,128)(2,1)} %copy-done.8) | copy-start | bytes 1572868
  172.1 32.0 %all-to-all-start.3 = ((bf16[1,32,12,1024]{3,2,0,1:T(8,128)(2,1)}), bf16[1,32,12,1024]{3,2,0,1:T(8,128)(2,1)S(1)}, u32[]{:S(2)}, u32[]{:S(2)}) async-start(bf16[1,32,12,1024]{3,2,0,1:T(8,128)(2,1)} %bitcast.10), calls=%async_computation.3 | async-start | bytes 2097152 | tf_op jit(solution)/shard_map/all_to_all | solution.py:21
  178.1 267.3 %all-reduce.3.cloned.1.call-start = ((), (), s32[]{:S(2)}) async-start(), calls=%async_computation.4 | async-start | bytes 262144 | tf_op jit(solution)/shard_map/psum | solution.py:104
Sparse Core Ops, SparseCore 0:
  184.5 260.8 all-reduce.2
where the time goes:
time: 454 us
  waiting for transfers between devices  282 us (62%)
  blocking collectives  95.7 us (21%)
  starting transfers between devices  26.3 us (6%)
  local copies, waits for them, and re-layouts  20.4 us (4%)
  between operations  14.4 us (3%)
  matrix products  7.95 us (2%)
  other arithmetic  7.16 us (2%)
    psum x1, waiting for transfers between devices, on_device(): router_grad = lax.psum(router_part, ('dp', 'tp', 'cp'))  237 us
    all_to_all x3, waiting for transfers between devices, trade(): lax.all_to_all(shaped, ('tp', 'cp'), split_axis=1, concat_axis=1, tiled=T...  44.8 us
    all_to_all x1, blocking collectives, trade(): lax.all_to_all(shaped, ('tp', 'cp'), split_axis=1, concat_axis=1, tiled=T...  33.6 us
    all_gather x1, blocking collectives, on_device(): lax.all_gather(down_weight[0], 'dp', axis=1, tiled=True)  27.5 us
    all_to_all x3, starting transfers between devices, trade(): lax.all_to_all(shaped, ('tp', 'cp'), split_axis=1, concat_axis=1, tiled=T...  26.3 us
    all_gather x1, blocking collectives, on_device(): lax.all_gather(gate_weight[0], 'dp', axis=0, tiled=True)  17.9 us
    all_gather x1, blocking collectives, on_device(): lax.all_gather(up_weight[0], 'dp', axis=0, tiled=True)  16.6 us
  transfers between devices with their start and end apart: 4, of which 3 were waited for; matrix products, arithmetic and copies ran while one was open for 3% of the time, Pallas kernels for 0%

commit v1 on v0

--- a/solution.py
+++ b/solution.py
@@ -2,6 +2,13 @@
 import jax.numpy as jnp
 from jax import lax
 from jax.sharding import PartitionSpec as P
+
+
+def swapped_in(value, axis, dim):
+    count = lax.axis_size(axis)
+    blocks = jnp.stack([value for _ in range(count)])
+    blocks = lax.all_to_all(blocks, axis, split_axis=0, concat_axis=0)
+    return jnp.concatenate(blocks, axis=dim)
 
 
 def route_slots(flat_ids, expert_count):
@@ -56,7 +63,7 @@
     contract = (((1,), (1,)), ((), ()))
     w_gate, w_up, w_down = (
         lax.all_gather(gate_weight[0], "dp", axis=0, tiled=True),
-        lax.all_gather(up_weight[0], "dp", axis=0, tiled=True),
+        swapped_in(up_weight[0], "dp", 0),
         lax.all_gather(down_weight[0], "dp", axis=1, tiled=True),
     )
     logits = jnp.dot(tokens, router_weight, preferred_element_type=jnp.float32)

time: 454 us -> 481 us (1.059)
  blocking collectives: 95.7 us -> 123 us
    all_to_all x1 -> x2, blocking collectives: 33.6 us -> 70.6 us  [trade(): lax.all_to_all(shaped, ('tp', 'cp'), split_axis=1, concat_axis=1, tiled=T...]
    all_gather x1 -> x0, blocking collectives: 16.6 us -> none  [on_device(): lax.all_gather(up_weight[0], 'dp', axis=0, tiled=True)]
    all_to_all x3 -> x2, starting transfers between devices: 26.3 us -> 10.9 us  [trade(): lax.all_to_all(shaped, ('tp', 'cp'), split_axis=1, concat_axis=1, tiled=T...]
    all_to_all x0 -> x1, starting transfers between devices: none -> 13.1 us  [swapped_in(): blocks = lax.all_to_all(blocks, axis, split_axis=0, concat_axis=0)]
    all_gather x1, blocking collectives: 27.5 us -> 35.3 us  [on_device(): lax.all_gather(down_weight[0], 'dp', axis=1, tiled=True)]
    all_to_all x3 -> x2, waiting for transfers between devices: 44.8 us -> 44.8 us  [trade(): lax.all_to_all(shaped, ('tp', 'cp'), split_axis=1, concat_axis=1, tiled=T...]
where the time goes in v1:
time: 481 us
  waiting for transfers between devices  284 us (59%)
  blocking collectives  123 us (26%)
  starting transfers between devices  24 us (5%)
  local copies, waits for them, and re-layouts  20.4 us (4%)
  between operations  14.5 us (3%)
  matrix products  7.96 us (2%)
  other arithmetic  7.34 us (2%)
    psum x1, waiting for transfers between devices, on_device(): router_grad = lax.psum(router_part, ('dp', 'tp', 'cp'))  239 us
    all_to_all x2, blocking collectives, trade(): lax.all_to_all(shaped, ('tp', 'cp'), split_axis=1, concat_axis=1, tiled=T...  70.6 us
    all_to_all x2, waiting for transfers between devices, trade(): lax.all_to_all(shaped, ('tp', 'cp'), split_axis=1, concat_axis=1, tiled=T...  44.8 us
    all_gather x1, blocking collectives, on_device(): lax.all_gather(down_weight[0], 'dp', axis=1, tiled=True)  35.3 us
    all_gather x1, blocking collectives, on_device(): lax.all_gather(gate_weight[0], 'dp', axis=0, tiled=True)  16.7 us
    all_to_all x1, starting transfers between devices, swapped_in(): blocks = lax.all_to_all(blocks, axis, split_axis=0, concat_axis=0)  13.1 us
    all_to_all x2, starting transfers between devices, trade(): lax.all_to_all(shaped, ('tp', 'cp'), split_axis=1, concat_axis=1, tiled=T...  10.9 us
  transfers between devices with their start and end apart: 4, of which 3 were waited for; matrix products, arithmetic and copies ran while one was open for 3% of the time, Pallas kernels for 0%

profile of v1, /device:TPU:1, one launch (start us, length us, event | category | flops | bytes accessed | tf_op | source)
XLA Modules:
  0.0 480.5 jit_solution(9443765154305707901)
XLA Ops:
  7.2 0.7 broadcast_multiply_fusion
  7.9 0.8 copy.57
  10.1 1.2 broadcast_in_dim.16
  11.6 1.9 scatter_custom_fusion
  13.7 37.2 %all_to_all.25 = bf16[1,32,12,1024]{3,2,0,1:T(8,128)(2,1)S(1)} all-to-all(bf16[1,32,12,1024]{3,2,0,1:T(8,128)(2,1)S(1)} %bitcast.71), channel_id=1, replica_groups=mesh['dp'=16,'tp'=4,'cp'=8] {'tp','cp'}, dimensions={1} | all-to-all | bytes 1572864 | tf_op jit(solution)/shard_map/all_to_all | solution.py:28
  50.9 1.0 stack.3
  51.9 13.1 %all-to-all-start.1 = ((bf16[16,64,384]{2,1,0:T(8,128)(2,1)}), bf16[16,64,384]{2,1,0:T(8,128)(2,1)S(1)}, u32[]{:S(2)}, u32[]{:S(2)}) async-start(bf16[16,64,384]{2,1,0:T(8,128)(2,1)} %stack.3), calls=%async_computation.1 | async-start | bytes 1572864 | tf_op jit(solution)/shard_map/all_to_all | solution.py:10
  65.0 35.3 %all-gather.1 = bf16[1,384,1024]{1,2,0:T(8,128)(2,1)} all-gather(bf16[1,384,64]{1,2,0:T(8,128)(2,1)S(1)} %copy-done.16), channel_id=3, replica_groups=mesh['dp'=16,'tp'=4,'cp'=8] {'dp'}, dimensions={2}, use_global_device_ids=true | all-gather | bytes 835584 | tf_op jit(solution)/shard_map/all_gather | solution.py:67
  100.3 16.7 %all-gather = bf16[1,1024,384]{2,1,0:T(8,128)(2,1)S(1)} all-gather(bf16[1,64,384]{2,1,0:T(8,128)(2,1)S(1)} %copy-done.17), channel_id=2, replica_groups=mesh['dp'=16,'tp'=4,'cp'=8] {'dp'}, dimensions={1}, use_global_device_ids=true | all-gather | bytes 835584 | tf_op jit(solution)/shard_map/all_gather | solution.py:65
  118.6 0.8 copy-done.10
  120.1 1.2 reshape_broadcast_in_dim.6
  121.3 4.8 %all-to-all-start.2 = ((bf16[1,32,12,1024]{3,2,0,1:T(8,128)(2,1)}), bf16[1,32,12,1024]{3,2,0,1:T(8,128)(2,1)S(1)}, u32[]{:S(2)}, u32[]{:S(2)}) async-start(bf16[1,32,12,1024]{3,2,0,1:T(8,128)(2,1)} %bitcast.9), calls=%async_computation.2 | async-start | bytes 2097152 | tf_op jit(solution)/shard_map/all_to_all | solution.py:28
  126.6 2.0 gather_fusion
  129.1 1.7 mul.98
  130.9 21.9 %all-to-all-done.2 = bf16[1,32,12,1024]{3,2,0,1:T(8,128)(2,1)S(1)} async-done(((bf16[1,32,12,1024]{3,2,0,1:T(8,128)(2,1)}), bf16[1,32,12,1024]{3,2,0,1:T(8,128)(2,1)S(1)}, u32[]{:S(2)}, u32[]{:S(2)}) %all-to-all-start.2) | async-done | bytes 786464 | tf_op jit(solution)/shard_map/all_to_all | solution.py:28
  153.0 1.2 gather_fusion.1
  154.6 1.1 fusion.10
  156.1 2.2 scatter_custom_fusion.1
  158.4 33.4 %all_to_all.26 = bf16[1,32,12,1024]{3,2,0,1:T(8,128)(2,1)S(1)} all-to-all(bf16[1,32,12,1024]{3,2,0,1:T(8,128)(2,1)S(1)} %bitcast.72), channel_id=1, replica_groups=mesh['dp'=16,'tp'=4,'cp'=8] {'tp','cp'}, dimensions={1} | all-to-all | bytes 1572864 | tf_op jit(solution)/shard_map/all_to_all | solution.py:28
  192.1 1.8 fusion.1
  193.9 0.7 fusion.4
  195.7 1.2 reshape_broadcast_in_dim.7
  196.8 6.0 %all-to-all-start.4 = ((bf16[1,32,12,1024]{3,2,0,1:T(8,128)(2,1)}), bf16[1,32,12,1024]{3,2,0,1:T(8,128)(2,1)S(1)}, u32[]{:S(2)}, u32[]{:S(2)}) async-start(bf16[1,32,12,1024]{3,2,0,1:T(8,128)(2,1)} %bitcast.11), calls=%async_computation.4 | async-start | bytes 2097152 | tf_op jit(solution)/shard_map/all_to_all | solution.py:28
  202.9 0.8 convolution_bitcast_fusion
  203.8 2.1 multiply_reduce_fusion
  205.9 22.9 %all-to-all-done.4 = bf16[1,32,12,1024]{3,2,0,1:T(8,128)(2,1)S(1)} async-done(((bf16[1,32,12,1024]{3,2,0,1:T(8,128)(2,1)}), bf16[1,32,12,1024]{3,2,0,1:T(8,128)(2,1)S(1)}, u32[]{:S(2)}, u32[]{:S(2)}) %all-to-all-start.4) | async-done | bytes 786464 | tf_op jit(solution)/shard_map/all_to_all | solution.py:28
  229.0 1.2 gather_fusion.2
  230.3 0.6 reshape.113
  230.9 1.2 reduce_sum.60
  232.2 1.0 fusion
  233.1 239.0 %all-reduce.3.cloned.1.call-done = f32[1024,32]{0,1:T(8,128)} async-done(((f32[1024,32]{0,1:T(8,128)}), f32[1024,32]{0,1:T(8,128)}) %all-reduce.3.cloned.1.call-update) | async-done | bytes 131088 | tf_op jit(solution)/shard_map/psum | solution.py:111
  472.1 1.6 copy.73
  (82 shorter events, 7.7 us)
Async XLA Ops:
  7.2 119.3 %copy-start = (bf16[1024,32]{0,1:T(8,128)(2,1)S(1)}, bf16[1024,32]{0,1:T(8,128)(2,1)}, u32[]{:S(2)}) copy-start(bf16[1024,32]{0,1:T(8,128)(2,1)} %param.11) | copy-start | bytes 196612
  13.5 37.4 %copy-start.15 = (bf16[1,64,384]{2,1,0:T(8,128)(2,1)S(1)}, bf16[1,64,384]{2,1,0:T(8,128)(2,1)}, u32[]{:S(2)}) copy-start(bf16[1,64,384]{2,1,0:T(8,128)(2,1)} %param.13) | copy-start | bytes 147460
  50.9 14.1 %copy-start.16 = (bf16[1,384,64]{1,2,0:T(8,128)(2,1)S(1)}, bf16[1,384,64]{1,2,0:T(8,128)(2,1)}, u32[]{:S(2)}) copy-start(bf16[1,384,64]{1,2,0:T(8,128)(2,1)} %param.14) | copy-start | bytes 147460
  50.9 49.4 %copy-start.17 = (bf16[1,64,384]{2,1,0:T(8,128)(2,1)S(1)}, bf16[1,64,384]{2,1,0:T(8,128)(2,1)}, u32[]{:S(2)}) copy-start(bf16[1,64,384]{2,1,0:T(8,128)(2,1)} %param.12) | copy-start | bytes 147460
  51.9 65.3 %all-to-all-start.1 = ((bf16[16,64,384]{2,1,0:T(8,128)(2,1)}), bf16[16,64,384]{2,1,0:T(8,128)(2,1)S(1)}, u32[]{:S(2)}, u32[]{:S(2)}) async-start(bf16[16,64,384]{2,1,0:T(8,128)(2,1)} %stack.3), calls=%async_computation.1 | async-start | bytes 1572864 | tf_op jit(solution)/shard_map/all_to_all | solution.py:10
  116.9 0.9 copy-start.4
  117.1 1.3 copy-start.2
  117.8 0.8 copy-start.12
  117.8 1.6 copy-start.6
  118.6 0.8 copy-start.10
  120.1 6.1 %copy-start.18 = (s32[128,2]{0,1:T(2,128)S(1)}, s32[128,2]{0,1:T(2,128)}, u32[]{:S(2)}) copy-start(s32[128,2]{0,1:T(2,128)} %param.10) | copy-start | bytes 3076
  121.3 5.1 %copy-start.7 = (bf16[128,1024]{1,0:T(8,128)(2,1)S(1)}, bf16[128,1024]{1,0:T(8,128)(2,1)}, u32[]{:S(2)}) copy-start(bf16[128,1024]{1,0:T(8,128)(2,1)} %param.9) | copy-start | bytes 786436
  121.3 31.6 %all-to-all-start.2 = ((bf16[1,32,12,1024]{3,2,0,1:T(8,128)(2,1)}), bf16[1,32,12,1024]{3,2,0,1:T(8,128)(2,1)S(1)}, u32[]{:S(2)}, u32[]{:S(2)}) async-start(bf16[1,32,12,1024]{3,2,0,1:T(8,128)(2,1)} %bitcast.9), calls=%async_computation.2 | async-start | bytes 2097152 | tf_op jit(solution)/shard_map/all_to_all | solution.py:28
  126.6 2.2 copy-start.14
  154.5 1.2 copy-start.8
  154.5 1.5 copy-start.1
  191.9 2.0 copy-start.5
  192.0 1.8 copy-start.11
  192.1 1.8 copy-start.13
  193.9 1.1 copy-start.3
  196.8 6.9 %copy-start.9 = (bf16[128,2,1024]{2,1,0:T(2,128)(2,1)S(1)}, bf16[128,2,1024]{2,1,0:T(2,128)(2,1)}, u32[]{:S(2)}) copy-start(bf16[128,2,1024]{2,1,0:T(2,128)(2,1)} %copy-done.8) | copy-start | bytes 1572868
  196.8 31.9 %all-to-all-start.4 = ((bf16[1,32,12,1024]{3,2,0,1:T(8,128)(2,1)}), bf16[1,32,12,1024]{3,2,0,1:T(8,128)(2,1)S(1)}, u32[]{:S(2)}, u32[]{:S(2)}) async-start(bf16[1,32,12,1024]{3,2,0,1:T(8,128)(2,1)} %bitcast.11), calls=%async_computation.4 | async-start | bytes 2097152 | tf_op jit(solution)/shard_map/all_to_all | solution.py:28
  202.8 269.3 %all-reduce.3.cloned.1.call-start = ((), (), s32[]{:S(2)}) async-start(), calls=%async_computation.5 | async-start | bytes 262144 | tf_op jit(solution)/shard_map/psum | solution.py:111
Sparse Core Ops, SparseCore 0:
  209.2 262.8 all-reduce.2
